TPU v7x, 32 devices: a whole 2x2x4 slice. The times are simulated.
32 devices in a mesh: row: 4 (over y, core), col: 8 (over z, x).
Axes of the slice: x: 2, y: 2, z: 4, core: 2. Of those that a mesh axis runs over, the one named last changes fastest.
Arguments:
- ainv_top: float32 [4096, 4096], P('row', 'col'), may hold values from -0.25 to 0.25
- par_struct: int32 [8, 16], replicated, may hold values from 0 to 31, as said below
- par_panel: float32 [8, 16, 128, 128], P('col', 'row'), may hold values from -6 to 6
- par_linv: float32 [8, 128, 128], P('col', 'row'), may hold values from -0.0625 to 0.0625
- par_dinv: float32 [8, 128, 128], P('col', 'row'), may hold values from -192 to 192
- kid_panel: float32 [16, 16, 128, 128], P('col', 'row'), may hold values from -6 to 6
- kid_upper: float32 [16, 128, 128], P('col', 'row'), may hold values from -6 to 6
- kid_linv: float32 [16, 128, 128], P('col', 'row'), may hold values from -0.0625 to 0.0625
- kid_dinv: float32 [16, 128, 128], P('col', 'row'), may hold values from -192 to 192
Outputs:
- par_offdiag: float32 [8, 16, 128, 128], P('col', 'row')
- par_diag: float32 [8, 128, 128], P('col', 'row')
- kid_offdiag: float32 [16, 16, 128, 128], P('col', 'row')
- kid_parent: float32 [16, 128, 128], P('col', 'row')
- kid_diag: float32 [16, 128, 128], P('col', 'row')
Inputs may be any that keep to these rules, and one draw needn't show every extreme that they name: `par_struct`: in every row, entries 2j and 2j + 1 are two different ancestors among j * 4 to (j + 1) * 4 - 1.
All inputs are finite; a program needn't handle non-finite values.
Results may differ from a plain program's by a relative error of at most 0.00014.
Values sent between devices are 32-bit elements; how exact they have to be, the bound alone decides.
No kernel may reach another device: no remote copies, remote signals or barrier semaphores. Data moves between devices by JAX's collectives and lax.ppermute only.
A program may use at most 128 MiB of HBM per device.

v0:
```python
import jax
import jax.numpy as jnp
from jax import lax
from jax.sharding import PartitionSpec as P

high = lax.Precision.HIGH
highest = lax.Precision.HIGHEST


def mm(spec, *operands, precision=high):
    return jnp.einsum(spec, *operands, precision=precision)


def on_device(
    ainv_top, par_struct, par_panel, par_linv, par_dinv, kid_panel, kid_upper, kid_linv, kid_dinv
):
    grid_rows = lax.axis_size("row")
    grid_cols = lax.axis_size("col")
    my_row = lax.axis_index("row")
    my_col = lax.axis_index("col")
    width = par_panel.shape[-1]
    band_rows = width // grid_rows
    slot_share = par_panel.shape[1]
    children = kid_panel.shape[0]
    pair_width = par_struct.shape[1] // grid_cols
    tile_rows = ainv_top.shape[0] // width
    tile_cols = ainv_top.shape[1] // width
    local_tiles = ainv_top.reshape(tile_rows, width, tile_cols, width)
    pick_rows = lax.dynamic_slice_in_dim(par_struct, my_row * slot_share, slot_share, 1)
    pick_cols = lax.dynamic_slice_in_dim(par_struct, my_col * pair_width, pair_width, 1)
    pick_rows = pick_rows - my_row * tile_rows
    pick_cols = pick_cols - my_col * tile_cols
    tiles = local_tiles[pick_rows[:, :, None], :, pick_cols[:, None, :], :]
    small = jnp.concatenate([par_linv, par_dinv, kid_upper, kid_linv, kid_dinv], axis=0)
    small = lax.all_gather(small, "row", axis=1, tiled=True)
    plinv, pdinv = (small[0], small[1])
    kupper = small[2 : 2 + children]
    klinv = small[2 + children : 2 + 2 * children]
    kdinv = small[2 + 2 * children :]
    panels = jnp.concatenate([par_panel, kid_panel], axis=0)
    every = lax.all_gather(panels, "row", axis=1, tiled=True)
    moved = lax.all_to_all(tiles, "col", 0, 0, tiled=True)
    every = every.reshape(1 + children, grid_cols, pair_width, width, width)
    prod = mm("cjkab,nckbd->njad", moved, every)
    par_off = -mm("jab,bc->jac", prod[0], plinv)
    par_hat = mm("jab,bc->jac", par_panel[0], plinv)
    kid_hat = mm("njab,nbc->njac", kid_panel, klinv)
    kuphat = mm("nab,nbc->nac", kupper, klinv)
    kid_sum = prod[1:] + mm("jab,nbc->njac", par_off, kupper)
    kid_off = -mm("njab,nbc->njac", kid_sum, klinv)
    diag_part = mm("jba,jbc->ac", par_hat, par_off)
    parent_part = mm("jba,njbc->nac", par_off, kid_hat)
    hat_part = mm("njba,njbc->nac", kid_hat, kid_off)
    inner = parent_part - mm("ab,nbc->nac", diag_part, kuphat)
    edge_part = mm("nba,nbc->nac", kuphat, inner) - hat_part
    parts = jnp.concatenate([diag_part[None], parent_part, edge_part], axis=0)
    parts = parts.reshape(1 + 2 * children, grid_rows, band_rows, width)
    parts = lax.all_to_all(parts, "row", 1, 1, tiled=True)
    sums = parts.sum(axis=1)
    par_pivot = mm("ba,bc,cd->ad", plinv, pdinv, plinv)
    kid_pivot = mm("nba,nbc,ncd->nad", klinv, kdinv, klinv)
    kid_pivot = kid_pivot + mm("nba,bc,ncd->nad", kuphat, par_pivot, kuphat)
    start = my_row * band_rows
    par_diag = lax.dynamic_slice_in_dim(par_pivot, start, band_rows, 0) - sums[0]
    kid_par = -(sums[1 : 1 + children] + mm("ab,nbc->nac", par_diag, kuphat))
    kid_diag = lax.dynamic_slice_in_dim(kid_pivot, start, band_rows, 1) + sums[1 + children :]
    return (par_off[None], par_diag[None], kid_off, kid_par, kid_diag)


def solution(mesh):
    placed = (
        P("row", "col"),
        P(),
        P("col", "row", None, None),
        P("col", "row", None),
        P("col", "row", None),
        P("col", "row", None, None),
        P("col", "row", None),
        P("col", "row", None),
        P("col", "row", None),
    )
    return jax.shard_map(
        on_device,
        mesh=mesh,
        in_specs=placed,
        out_specs=(
            P("col", "row", None, None),
            P("col", "row", None),
            P("col", "row", None, None),
            P("col", "row", None),
            P("col", "row", None),
        ),
        check_vma=False,
    )
```

profile of v0, /device:TPU:0, one launch (start us, length us, event | category | flops | bytes accessed | tf_op | source)
XLA Modules:
  0.0 147.9 jit_solution(1128994719983951276)
XLA Ops:
  7.2 0.8 fusion.41
  7.9 0.8 fusion.43
  8.9 2.9 %reshape.58 = f32[8,128,4,128]{3,2,1,0:T(4,128)} reshape(f32[1024,512]{1,0:T(8,128)} %param.9) | data formatting | bytes 4194304 | tf_op jit(solution)/shard_map/reshape | solution.py:28
  11.8 1.9 %copy.49 = f32[8,128,4,128]{3,1,2,0:T(8,128)S(1)} copy(f32[8,128,4,128]{3,2,1,0:T(4,128)} %reshape.58) | data formatting | bytes 4194304 | tf_op jit(solution)/shard_map/reshape | solution.py:28
  13.7 2.9 %gather_fusion = f32[64,128,128]{2,1,0:T(8,128)} fusion(f32[8,128,4,128]{3,1,2,0:T(8,128)S(1)} %copy.49, s32[64]{0:T(128)S(1)} %reshape.36), kind=kCustom, calls=%fused_computation | custom fusion | bytes 8389120 | tf_op jit(solution)/shard_map/gather | solution.py:33
  16.6 7.4 %all-to-all-start = ((f32[8,4,2,128,128]{4,3,2,1,0:T(8,128)}), f32[8,4,2,128,128]{4,3,2,1,0:T(8,128)}, u32[]{:S(2)}, u32[]{:S(2)}) async-start(f32[8,4,2,128,128]{4,3,2,1,0:T(8,128)} %bitcast.134), calls=%async_computation | async-start | bytes 8388608 | tf_op jit(solution)/shard_map/all_to_all | solution.py:42
  24.0 1.0 pad_maximum_fusion
  25.1 7.2 %all_gather.7 = f32[8,128,128]{2,1,0:T(8,128)S(1)} all-gather(f32[8,32,128]{2,1,0:T(8,128)S(1)} %constant_dynamic-update-slice_fusion), channel_id=1, replica_groups=mesh['row'=4,'col'=8] {'row'}, dimensions={1}, use_global_device_ids=true | all-gather | bytes 655360 | tf_op jit(solution)/shard_map/all_gather | solution.py:35
  33.3 0.3 convolution_bitcast_fusion.2
  34.0 0.4 convolution_bitcast_fusion.1
  34.4 22.1 %all-gather.2.cloned.1.call-done = f32[3,16,128,128]{3,2,1,0:T(8,128)} async-done(((f32[3,4,128,128]{3,2,1,0:T(8,128)}), f32[3,16,128,128]{3,2,1,0:T(8,128)}) %all-gather.2.cloned.1.call-update) | async-done | bytes 3145744 | tf_op jit(solution)/shard_map/all_gather | solution.py:41
  56.5 60.8 %all-to-all-done = f32[8,4,2,128,128]{4,3,2,1,0:T(8,128)} async-done(((f32[8,4,2,128,128]{4,3,2,1,0:T(8,128)}), f32[8,4,2,128,128]{4,3,2,1,0:T(8,128)}, u32[]{:S(2)}, u32[]{:S(2)}) %all-to-all-start) | async-done | bytes 4194336 | tf_op jit(solution)/shard_map/all_to_all | solution.py:42
  117.3 7.8 %fusion.3 = f32[3,4,128,128]{2,3,1,0:T(8,128)S(1)} fusion(f32[3,8,2,128,128,1]{4,3,2,1,5,0:T(8,128)} %bitcast.136, f32[8,4,2,128,128]{4,3,2,1,0:T(8,128)} %all-to-all-done), kind=kOutput, calls=%fused_computation.4 | convolution fusion | flops 2415919104 | bytes 8126464 | tf_op jit(solution)/shard_map/cjkab,nckbd->njad/dot_general | solution.py:11
  125.1 0.4 convolution_negate_fusion.1
  125.5 0.4 fusion.6
  126.0 0.4 fusion.11
  126.6 0.6 convolution_negate_fusion
  127.2 0.4 convolution_bitcast_fusion.3
  128.1 0.7 pad_maximum_fusion.1
  128.8 3.5 %all-to-all-start.1 = ((f32[5,4,32,128]{3,2,0,1:T(8,128)}), f32[5,4,32,128]{3,2,0,1:T(8,128)S(1)}, u32[]{:S(2)}, u32[]{:S(2)}) async-start(f32[5,4,32,128]{3,2,0,1:T(8,128)} %pad_maximum_fusion.1), calls=%async_computation.1 | async-start | bytes 655360 | tf_op jit(solution)/shard_map/all_to_all | solution.py:58
  132.7 6.3 %all-to-all-done.1 = f32[5,4,32,128]{3,2,0,1:T(8,128)S(1)} async-done(((f32[5,4,32,128]{3,2,0,1:T(8,128)}), f32[5,4,32,128]{3,2,0,1:T(8,128)S(1)}, u32[]{:S(2)}, u32[]{:S(2)}) %all-to-all-start.1) | async-done | bytes 327712 | tf_op jit(solution)/shard_map/all_to_all | solution.py:58
  139.0 0.8 fusion.9
  139.8 0.6 fusion.39
  140.4 0.6 slice_add_fusion
  (38 shorter events, 2.8 us)
Async XLA Ops:
  16.5 7.5 %copy-start.1 = (f32[2,4,128,128]{3,2,1,0:T(8,128)S(1)}, f32[2,4,128,128]{3,2,1,0:T(8,128)}, u32[]{:S(2)}) copy-start(f32[2,4,128,128]{3,2,1,0:T(8,128)} %param.14) | copy-start | bytes 1572868
  16.5 7.5 %copy-start.3 = (f32[1,4,128,128]{3,2,1,0:T(8,128)S(1)}, f32[1,4,128,128]{3,2,1,0:T(8,128)}, u32[]{:S(2)}) copy-start(f32[1,4,128,128]{3,2,1,0:T(8,128)} %param.11) | copy-start | bytes 786436
  16.5 8.5 %copy-start.7 = (f32[1,32,128]{2,1,0:T(8,128)S(1)}, f32[1,32,128]{2,1,0:T(8,128)}, u32[]{:S(2)}) copy-start(f32[1,32,128]{2,1,0:T(8,128)} %param.12) | copy-start | bytes 49156
  16.5 8.5 %copy-start.8 = (f32[1,32,128]{2,1,0:T(8,128)S(1)}, f32[1,32,128]{2,1,0:T(8,128)}, u32[]{:S(2)}) copy-start(f32[1,32,128]{2,1,0:T(8,128)} %param.13) | copy-start | bytes 49156
  16.5 8.5 %copy-start.4 = (f32[2,32,128]{2,1,0:T(8,128)S(1)}, f32[2,32,128]{2,1,0:T(8,128)}, u32[]{:S(2)}) copy-start(f32[2,32,128]{2,1,0:T(8,128)} %param.15) | copy-start | bytes 98308
  16.6 8.5 %copy-start.5 = (f32[2,32,128]{2,1,0:T(8,128)S(1)}, f32[2,32,128]{2,1,0:T(8,128)}, u32[]{:S(2)}) copy-start(f32[2,32,128]{2,1,0:T(8,128)} %param.16) | copy-start | bytes 98308
  16.6 8.5 %copy-start.6 = (f32[2,32,128]{2,1,0:T(8,128)S(1)}, f32[2,32,128]{2,1,0:T(8,128)}, u32[]{:S(2)}) copy-start(f32[2,32,128]{2,1,0:T(8,128)} %param.17) | copy-start | bytes 98308
  16.6 100.7 %all-to-all-start = ((f32[8,4,2,128,128]{4,3,2,1,0:T(8,128)}), f32[8,4,2,128,128]{4,3,2,1,0:T(8,128)}, u32[]{:S(2)}, u32[]{:S(2)}) async-start(f32[8,4,2,128,128]{4,3,2,1,0:T(8,128)} %bitcast.134), calls=%async_computation | async-start | bytes 8388608 | tf_op jit(solution)/shard_map/all_to_all | solution.py:42
  24.0 32.5 %all-gather.2.cloned.1.call-start = ((), (), s32[]{:S(2)}) async-start(), calls=%async_computation.2 | async-start | bytes 3932160 | tf_op jit(solution)/shard_map/all_gather | solution.py:41
  125.5 7.2 %copy-start = (f32[4,128,128]{2,1,0:T(8,128)}, f32[4,128,128]{2,1,0:T(8,128)S(1)}, u32[]{:S(2)}) copy-start(f32[4,128,128]{2,1,0:T(8,128)S(1)} %convolution_negate_fusion.1) | copy-start | bytes 786436
  127.2 13.8 %copy-start.2 = (f32[2,4,128,128]{3,2,1,0:T(8,128)}, f32[2,4,128,128]{3,2,1,0:T(8,128)S(1)}, u32[]{:S(2)}) copy-start(f32[2,4,128,128]{3,2,1,0:T(8,128)S(1)} %convolution_negate_fusion) | copy-start | bytes 1572868
  128.8 10.2 %all-to-all-start.1 = ((f32[5,4,32,128]{3,2,0,1:T(8,128)}), f32[5,4,32,128]{3,2,0,1:T(8,128)S(1)}, u32[]{:S(2)}, u32[]{:S(2)}) async-start(f32[5,4,32,128]{3,2,0,1:T(8,128)} %pad_maximum_fusion.1), calls=%async_computation.1 | async-start | bytes 655360 | tf_op jit(solution)/shard_map/all_to_all | solution.py:58
Sparse Core Ops, SparseCore 0:
  26.4 30.0 all-gather.1
where the time goes:
time: 148 us
  waiting for transfers between devices  89.2 us (60%)
  between operations  14.3 us (10%)
  matrix products  13.9 us (9%)
  starting transfers between devices  10.9 us (7%)
  local copies, waits for them, and re-layouts  7.82 us (5%)
  blocking collectives  7.2 us (5%)
  other arithmetic  4.55 us (3%)
    all_to_all x1, waiting for transfers between devices, on_device(): moved = lax.all_to_all(tiles, 'col', 0, 0, tiled=True)  60.8 us
    all_gather x1, waiting for transfers between devices, on_device(): every = lax.all_gather(panels, 'row', axis=1, tiled=True)  22.1 us
    dot_general x19, matrix products, mm(): return jnp.einsum(spec, *operands, precision=precision)  13.9 us
    all_to_all x1, starting transfers between devices, on_device(): moved = lax.all_to_all(tiles, 'col', 0, 0, tiled=True)  7.4 us
    all_gather x1, blocking collectives, on_device(): small = lax.all_gather(small, 'row', axis=1, tiled=True)  7.2 us
    all_to_all x1, waiting for transfers between devices, on_device(): parts = lax.all_to_all(parts, 'row', 1, 1, tiled=True)  6.27 us
    reshape x2, local copies, waits for them, and re-layouts, on_device(): local_tiles = ainv_top.reshape(tile_rows, width, tile_cols, width)  4.78 us
    all_to_all x1, starting transfers between devices, on_device(): parts = lax.all_to_all(parts, 'row', 1, 1, tiled=True)  3.45 us
  transfers between devices with their start and end apart: 3, of which 3 were waited for; matrix products, arithmetic and copies ran while one was open for 2% of the time, Pallas kernels for 0%

commit v1 on v0

--- a/solution.py
+++ b/solution.py
@@ -38,7 +38,12 @@
     klinv = small[2 + children : 2 + 2 * children]
     kdinv = small[2 + 2 * children :]
     panels = jnp.concatenate([par_panel, kid_panel], axis=0)
-    every = lax.all_gather(panels, "row", axis=1, tiled=True)
+    ring = [panels]
+    for hop in range(3):
+        ring.append(lax.ppermute(ring[-1], "row", [(dev, (dev + 1) % 4) for dev in range(4)]))
+    every = jnp.roll(
+        jnp.concatenate(ring[::-1], axis=1), (lax.axis_index("row") + 1) * ring[0].shape[1], axis=1
+    )
     moved = lax.all_to_all(tiles, "col", 0, 0, tiled=True)
     every = every.reshape(1 + children, grid_cols, pair_width, width, width)
     prod = mm("cjkab,nckbd->njad", moved, every)

time: 148 us -> 133 us (0.90)
  waiting for transfers between devices: 89.2 us -> 75.8 us
  between operations: 14.3 us -> 1.12 us
  blocking collectives: 7.2 us -> 15.1 us
  local copies, waits for them, and re-layouts: 7.82 us -> 10.8 us
  other arithmetic: 4.55 us -> 2.31 us
  matrix products: 13.9 us -> 16.1 us
    all_gather x1 -> x0, waiting for transfers between devices: 22.1 us -> none  [on_device(): every = lax.all_gather(panels, 'row', axis=1, tiled=True)]
    ppermute x0 -> x3, waiting for transfers between devices: none -> 19.2 us  [on_device(): lax.ppermute(ring[-1], 'row', [(dev, (dev + 1) % 4) for dev in range(4)])]
    all_to_all x1, waiting for transfers between devices: 60.8 us -> 51.2 us  [on_device(): moved = lax.all_to_all(tiles, 'col', 0, 0, tiled=True)]
    all_gather x1, blocking collectives: 7.2 us -> 15.1 us  [on_device(): small = lax.all_gather(small, 'row', axis=1, tiled=True)]
    unnamed x22 -> x47, local copies, waits for them, and re-layouts: 0.06 us -> 2.79 us
    dot_general x19, matrix products: 13.9 us -> 16.1 us  [mm(): return jnp.einsum(spec, *operands, precision=precision)]
  transfers between devices with their start and end apart: 3 -> 5, of which waited for: 3 -> 4; matrix products, arithmetic and copies ran while one was open for 2% -> 6% of each run, Pallas kernels for 0% -> 0%
where the time goes in v1:
time: 133 us; the launch traced here: 132 us
  waiting for transfers between devices  75.8 us (57%)
  matrix products  16.1 us (12%)
  blocking collectives  15.1 us (11%)
  starting transfers between devices  11.1 us (8%)
  local copies, waits for them, and re-layouts  10.8 us (8%)
  other arithmetic  2.31 us (2%)
    all_to_all x1, waiting for transfers between devices, on_device(): moved = lax.all_to_all(tiles, 'col', 0, 0, tiled=True)  51.2 us
    ppermute x3, waiting for transfers between devices, on_device(): lax.ppermute(ring[-1], 'row', [(dev, (dev + 1) % 4) for dev in range(4)])  19.2 us
    dot_general x19, matrix products, mm(): return jnp.einsum(spec, *operands, precision=precision)  16.1 us
    all_gather x1, blocking collectives, on_device(): small = lax.all_gather(small, 'row', axis=1, tiled=True)  15.1 us
    all_to_all x1, starting transfers between devices, on_device(): moved = lax.all_to_all(tiles, 'col', 0, 0, tiled=True)  7.4 us
    all_to_all x1, waiting for transfers between devices, on_device(): parts = lax.all_to_all(parts, 'row', 1, 1, tiled=True)  5.36 us
    reshape x2, local copies, waits for them, and re-layouts, on_device(): local_tiles = ainv_top.reshape(tile_rows, width, tile_cols, width)  4.76 us
    all_to_all x1, starting transfers between devices, on_device(): parts = lax.all_to_all(parts, 'row', 1, 1, tiled=True)  3.45 us
  transfers between devices with their start and end apart: 5, of which 4 were waited for; matrix products, arithmetic and copies ran while one was open for 6% of the time, Pallas kernels for 0%

profile of v1, /device:TPU:0, one launch (start us, length us, event | category | flops | bytes accessed | tf_op | source)
XLA Modules:
  0.0 132.4 jit_solution(9866398177197892345)
XLA Ops:
  0.6 2.9 %reshape.58 = f32[8,128,4,128]{3,2,1,0:T(4,128)} reshape(f32[1024,512]{1,0:T(8,128)} %param.9) | data formatting | bytes 4194304 | tf_op jit(solution)/shard_map/reshape | solution.py:28
  3.5 1.9 %copy.49 = f32[8,128,4,128]{3,1,2,0:T(8,128)S(1)} copy(f32[8,128,4,128]{3,2,1,0:T(4,128)} %reshape.58) | data formatting | bytes 4194304 | tf_op jit(solution)/shard_map/reshape | solution.py:28
  5.8 2.9 %gather_fusion = f32[64,128,128]{2,1,0:T(8,128)} fusion(f32[8,128,4,128]{3,1,2,0:T(8,128)S(1)} %copy.49, s32[64]{0:T(128)S(1)} %reshape.36), kind=kCustom, calls=%fused_computation | custom fusion | bytes 8389120 | tf_op jit(solution)/shard_map/gather | solution.py:33
  8.7 7.4 %all-to-all-start = ((f32[8,4,2,128,128]{4,3,2,1,0:T(8,128)}), f32[8,4,2,128,128]{4,3,2,1,0:T(8,128)}, u32[]{:S(2)}, u32[]{:S(2)}) async-start(f32[8,4,2,128,128]{4,3,2,1,0:T(8,128)} %bitcast.134), calls=%async_computation | async-start | bytes 8388608 | tf_op jit(solution)/shard_map/all_to_all | solution.py:47
  16.4 11.3 %collective-permute-done = f32[3,4,128,128]{3,2,1,0:T(8,128)S(1)} collective-permute-done((f32[3,4,128,128]{3,2,1,0:T(8,128)S(1)}, f32[3,4,128,128]{3,2,1,0:T(8,128)S(1)}, u32[]{:S(2)}, u32[]{:S(2)}) %collective-permute-start) | collective-permute-done | bytes 786464 | tf_op jit(solution)/shard_map/ppermute | solution.py:43
  27.6 15.1 %all_gather.3 = f32[8,128,128]{2,1,0:T(8,128)S(1)} all-gather(f32[8,32,128]{2,1,0:T(8,128)S(1)} %constant_dynamic-update-slice_fusion.10), channel_id=1, replica_groups=mesh['row'=4,'col'=8] {'row'}, dimensions={1}, use_global_device_ids=true | all-gather | bytes 655360 | tf_op jit(solution)/shard_map/all_gather | solution.py:35
  43.7 0.9 fusion.25
  45.0 0.9 fusion.17
  45.9 1.2 convolution_bitcast_fusion.1
  47.1 7.9 %collective-permute-done.2 = f32[3,4,128,128]{3,2,1,0:T(8,128)} collective-permute-done((f32[3,4,128,128]{3,2,1,0:T(8,128)S(1)}, f32[3,4,128,128]{3,2,1,0:T(8,128)}, u32[]{:S(2)}, u32[]{:S(2)}) %collective-permute-start.2) | collective-permute-done | bytes 786464 | tf_op jit(solution)/shard_map/ppermute | solution.py:43
  55.1 1.2 constant_dynamic-update-slice_fusion.9
  56.5 1.2 constant_dynamic-update-slice_fusion.4
  58.1 51.2 %all-to-all-done = f32[8,4,2,128,128]{4,3,2,1,0:T(8,128)} async-done(((f32[8,4,2,128,128]{4,3,2,1,0:T(8,128)}), f32[8,4,2,128,128]{4,3,2,1,0:T(8,128)}, u32[]{:S(2)}, u32[]{:S(2)}) %all-to-all-start) | async-done | bytes 4194336 | tf_op jit(solution)/shard_map/all_to_all | solution.py:47
  109.4 7.0 %fusion.3 = f32[3,4,128,128]{2,3,1,0:T(8,128)S(1)} fusion(f32[3,8,2,128,128,1]{4,3,2,1,5,0:T(8,128)S(1)} %bitcast.135, f32[8,4,2,128,128]{4,3,2,1,0:T(8,128)} %all-to-all-done), kind=kOutput, calls=%fused_computation.4 | convolution fusion | flops 2415919104 | bytes 8126464 | tf_op jit(solution)/shard_map/cjkab,nckbd->njad/dot_general | solution.py:11
  116.8 0.4 fusion.6
  117.6 0.4 fusion.11
  118.0 0.6 convolution_negate_fusion
  119.5 0.8 pad_maximum_fusion.1
  120.2 3.5 %all-to-all-start.1 = ((f32[5,4,32,128]{3,2,0,1:T(8,128)}), f32[5,4,32,128]{3,2,0,1:T(8,128)S(1)}, u32[]{:S(2)}, u32[]{:S(2)}) async-start(f32[5,4,32,128]{3,2,0,1:T(8,128)} %pad_maximum_fusion.1), calls=%async_computation.1 | async-start | bytes 655360 | tf_op jit(solution)/shard_map/all_to_all | solution.py:63
  123.9 1.1 fusion.19
  125.0 5.4 %all-to-all-done.1 = f32[5,4,32,128]{3,2,0,1:T(8,128)S(1)} async-done(((f32[5,4,32,128]{3,2,0,1:T(8,128)}), f32[5,4,32,128]{3,2,0,1:T(8,128)S(1)}, u32[]{:S(2)}, u32[]{:S(2)}) %all-to-all-start.1) | async-done | bytes 327712 | tf_op jit(solution)/shard_map/all_to_all | solution.py:63
  130.4 0.6 fusion.39
  131.0 0.8 fusion.9
  131.8 0.6 slice_add_fusion
  (68 shorter events, 4.1 us)
Async XLA Ops:
  0.6 4.8 %copy-start.16 = (s32[8,16]{1,0:T(8,128)S(1)}, s32[8,16]{1,0:T(8,128)}, u32[]{:S(2)}) copy-start(s32[8,16]{1,0:T(8,128)} %param.10) | copy-start | bytes 1540
  8.7 7.4 %copy-start.2 = (f32[2,4,128,128]{3,2,1,0:T(8,128)S(1)}, f32[2,4,128,128]{3,2,1,0:T(8,128)}, u32[]{:S(2)}) copy-start(f32[2,4,128,128]{3,2,1,0:T(8,128)} %param.14) | copy-start | bytes 1572868
  8.7 7.4 %copy-start.5 = (f32[1,4,128,128]{3,2,1,0:T(8,128)S(1)}, f32[1,4,128,128]{3,2,1,0:T(8,128)}, u32[]{:S(2)}) copy-start(f32[1,4,128,128]{3,2,1,0:T(8,128)} %param.11) | copy-start | bytes 786436
  8.7 7.6 %copy-start.14 = (f32[1,32,128]{2,1,0:T(8,128)S(1)}, f32[1,32,128]{2,1,0:T(8,128)}, u32[]{:S(2)}) copy-start(f32[1,32,128]{2,1,0:T(8,128)} %param.12) | copy-start | bytes 49156
  8.7 7.6 %copy-start.15 = (f32[1,32,128]{2,1,0:T(8,128)S(1)}, f32[1,32,128]{2,1,0:T(8,128)}, u32[]{:S(2)}) copy-start(f32[1,32,128]{2,1,0:T(8,128)} %param.13) | copy-start | bytes 49156
  8.7 7.6 %copy-start.11 = (f32[2,32,128]{2,1,0:T(8,128)S(1)}, f32[2,32,128]{2,1,0:T(8,128)}, u32[]{:S(2)}) copy-start(f32[2,32,128]{2,1,0:T(8,128)} %param.15) | copy-start | bytes 98308
  8.7 7.6 %copy-start.12 = (f32[2,32,128]{2,1,0:T(8,128)S(1)}, f32[2,32,128]{2,1,0:T(8,128)}, u32[]{:S(2)}) copy-start(f32[2,32,128]{2,1,0:T(8,128)} %param.16) | copy-start | bytes 98308
  8.7 7.6 %copy-start.13 = (f32[2,32,128]{2,1,0:T(8,128)S(1)}, f32[2,32,128]{2,1,0:T(8,128)}, u32[]{:S(2)}) copy-start(f32[2,32,128]{2,1,0:T(8,128)} %param.17) | copy-start | bytes 98308
  8.7 100.7 %all-to-all-start = ((f32[8,4,2,128,128]{4,3,2,1,0:T(8,128)}), f32[8,4,2,128,128]{4,3,2,1,0:T(8,128)}, u32[]{:S(2)}, u32[]{:S(2)}) async-start(f32[8,4,2,128,128]{4,3,2,1,0:T(8,128)} %bitcast.134), calls=%async_computation | async-start | bytes 8388608 | tf_op jit(solution)/shard_map/all_to_all | solution.py:47
  16.2 11.5 %collective-permute-start = (f32[3,4,128,128]{3,2,1,0:T(8,128)S(1)}, f32[3,4,128,128]{3,2,1,0:T(8,128)S(1)}, u32[]{:S(2)}, u32[]{:S(2)}) collective-permute-start(f32[3,4,128,128]{3,2,1,0:T(8,128)S(1)} %pad_maximum_fusion), channel_id=1, source_target_pairs={{0,8},{8,16},{16,24},{24,0},{1,9},{9,17},{17,25},{25,1},{2,10},{10... | collective-permute-start | bytes 2359304 | tf_op jit(solution)/shard_map/ppermute | solution.py:43
  27.6 15.9 %collective-permute-start.1 = (f32[3,4,128,128]{3,2,1,0:T(8,128)S(1)}, f32[3,4,128,128]{3,2,1,0:T(8,128)S(1)}, u32[]{:S(2)}, u32[]{:S(2)}) collective-permute-start(f32[3,4,128,128]{3,2,1,0:T(8,128)S(1)} %collective-permute-done), channel_id=1, source_target_pairs={{0,8},{8,16},{16,24},{24,0},{1,9},{9,17},{17,25},{25,1},{2,10},{10... | collective-permute-start | bytes 2359304 | tf_op jit(solution)/shard_map/ppermute | solution.py:43
  42.8 15.0 %copy-start = (f32[8,128,128]{2,1,0:T(8,128)}, f32[8,128,128]{2,1,0:T(8,128)S(1)}, u32[]{:S(2)}) copy-start(f32[8,128,128]{2,1,0:T(8,128)S(1)} %all_gather.3) | copy-start | bytes 1572868
  43.3 14.5 %copy-start.9 = (f32[128,128]{1,0:T(8,128)}, f32[128,128]{1,0:T(8,128)S(1)}, u32[]{:S(2)}) copy-start(f32[128,128]{1,0:T(8,128)S(1)} %fusion.30) | copy-start | bytes 196612
  43.5 11.6 %collective-permute-start.2 = (f32[3,4,128,128]{3,2,1,0:T(8,128)S(1)}, f32[3,4,128,128]{3,2,1,0:T(8,128)}, u32[]{:S(2)}, u32[]{:S(2)}) collective-permute-start(f32[3,4,128,128]{3,2,1,0:T(8,128)S(1)} %collective-permute-done.1), channel_id=1, source_target_pairs={{0,8},{8,16},{16,24},{24,0},{1,9},{9,17},{17,25},{25,1},{2,10},{10... | collective-permute-start | bytes 2359304 | tf_op jit(solution)/shard_map/ppermute | solution.py:43
  109.4 7.0 %copy-start.1 = (f32[8,128,128]{2,1,0:T(8,128)S(1)}, f32[8,128,128]{2,1,0:T(8,128)}, u32[]{:S(2)}) copy-start(f32[8,128,128]{2,1,0:T(8,128)} %copy-done) | copy-start | bytes 1572868
  109.4 8.2 %copy-start.3 = (f32[2,4,128,128]{2,3,1,0:T(8,128)S(1)}, f32[2,4,128,128]{2,3,1,0:T(8,128)}, u32[]{:S(2)}) copy-start(f32[2,4,128,128]{2,3,1,0:T(8,128)} %convolution_bitcast_fusion.1) | copy-start | bytes 1572868
  116.4 7.3 %copy-start.7 = (f32[128,2,128]{0,2,1:T(8,128)S(1)}, f32[128,2,128]{0,2,1:T(8,128)}, u32[]{:S(2)}) copy-start(f32[128,2,128]{0,2,1:T(8,128)} %fusion.25) | copy-start | bytes 393220
  116.4 7.5 %copy-start.8 = (f32[2,128,128]{1,2,0:T(8,128)S(1)}, f32[2,128,128]{1,2,0:T(8,128)}, u32[]{:S(2)}) copy-start(f32[2,128,128]{1,2,0:T(8,128)} %fusion.17) | copy-start | bytes 393220
  116.4 14.0 %copy-start.10 = (f32[128,128]{1,0:T(8,128)S(1)}, f32[128,128]{1,0:T(8,128)}, u32[]{:S(2)}) copy-start(f32[128,128]{1,0:T(8,128)} %copy-done.9) | copy-start | bytes 196612
  116.8 15.6 %copy-start.4 = (f32[4,128,128]{2,1,0:T(8,128)}, f32[4,128,128]{2,1,0:T(8,128)S(1)}, u32[]{:S(2)}) copy-start(f32[4,128,128]{2,1,0:T(8,128)S(1)} %convolution_negate_fusion.1) | copy-start | bytes 786436
  118.6 13.9 %copy-start.6 = (f32[2,4,128,128]{3,2,1,0:T(8,128)}, f32[2,4,128,128]{3,2,1,0:T(8,128)S(1)}, u32[]{:S(2)}) copy-start(f32[2,4,128,128]{3,2,1,0:T(8,128)S(1)} %convolution_negate_fusion) | copy-start | bytes 1572868
  120.2 10.2 %all-to-all-start.1 = ((f32[5,4,32,128]{3,2,0,1:T(8,128)}), f32[5,4,32,128]{3,2,0,1:T(8,128)S(1)}, u32[]{:S(2)}, u32[]{:S(2)}) async-start(f32[5,4,32,128]{3,2,0,1:T(8,128)} %pad_maximum_fusion.1), calls=%async_computation.1 | async-start | bytes 655360 | tf_op jit(solution)/shard_map/all_to_all | solution.py:63
